TPU v7x, 32 devices: a whole 2x2x4 slice. The times are simulated.
32 devices in a mesh: groups: 2 (over x), region: 16 (over z, y, core).
Axes of the slice: x: 2, y: 2, z: 4, core: 2. Of those that a mesh axis runs over, the one named last changes fastest.
Arguments:
- record: bfloat16 [16384, 640], P(('groups', 'region')), parts along dimension 0, may hold values from -6 to 6
- target: bfloat16 [4, 16384, 8192], P(None, ('groups', 'region')), parts along dimension 1, may hold values from -0.59765625 to 0.59765625
- offset: int32 [2], P('groups'), parts along dimension 0, may hold values from 0 to 127
- lag_steps: int32 [6], P('groups'), parts along dimension 0, may hold values from 1 to 8
Outputs:
- grad: float32 [16384, 640], P(('groups', 'region')), parts along dimension 0
There are 2 independent parts, one for each index of `groups`. A program takes and returns all parts, laid end to end along the dimension named above; each array names one. Nothing has to cross between parts.
All inputs are finite; a program needn't handle non-finite values.
Results may differ from a plain program's by a relative error of at most 0.0005.
Values may be sent and summed in bfloat16 or wider, within the bound.
A program may use at most 256 MiB of HBM per device.

v0:
```python
import jax
import jax.numpy as jnp
from jax import lax
from jax.sharding import PartitionSpec as P

REGIONS = 8192
SAMPLES = 384
SLACK = 128
LAGS = 3


def shifted(value, axis, steps):
    count = lax.axis_size(axis)
    pairs = [(source, (source + steps) % count) for source in range(count)]
    return lax.ppermute(value, axis, pairs)


def outer_dot(left, right):
    return lax.dot_general(
        left, right, (((1,), (1,)), ((), ())), preferred_element_type=jnp.float32
    )


def split_views(window, lag_steps):
    early_view = window[:, :SAMPLES]
    later_list = []
    for lag_number in range(LAGS):
        later_list.append(lax.dynamic_slice_in_dim(window, lag_steps[lag_number], SAMPLES, 1))
    return (early_view, jnp.stack(later_list))


def place_views(early_part, later_parts, lag_steps, win_width):
    block_rows = early_part.shape[0]
    placed = jnp.pad(early_part, ((0, 0), (0, win_width - SAMPLES)))
    blank = jnp.zeros((block_rows, win_width), jnp.float32)
    for lag_number in range(LAGS):
        placed = placed + lax.dynamic_update_slice(
            blank, later_parts[lag_number], (0, lag_steps[lag_number])
        )
    return placed


def pair_tiles(own_views, other_views, target, flipped, column_at, width, factor):
    inverse = 1.0 / SAMPLES
    weight = SAMPLES / REGIONS
    own_early, own_later = own_views
    other_early, other_later = other_views
    tiles = lax.dynamic_slice_in_dim(target, column_at, width, 2).astype(jnp.float32)
    mirror = lax.dynamic_slice_in_dim(flipped, column_at, width, 2).astype(jnp.float32)
    cov_zero = outer_dot(own_early, other_early) * inverse
    cov_fore = (
        jnp.einsum("rs,lcs->lrc", own_early, other_later, preferred_element_type=jnp.float32)
        * inverse
    )
    cov_back = (
        jnp.einsum("lrs,cs->lrc", own_later, other_early, preferred_element_type=jnp.float32)
        * inverse
    )
    sym_err = (weight * (2.0 * cov_zero - tiles[0] - mirror[0]) * factor).astype(jnp.bfloat16)
    fore_err = (weight * (cov_fore - tiles[1:]) * factor).astype(jnp.bfloat16)
    back_err = (weight * (cov_back - mirror[1:]) * factor).astype(jnp.bfloat16)
    return (sym_err, fore_err, back_err)


def own_terms(errors, other_views):
    sym_err, fore_err, back_err = errors
    other_early, other_later = other_views
    to_early = jnp.dot(sym_err, other_early, preferred_element_type=jnp.float32)
    to_early = to_early + jnp.einsum(
        "lrc,lcs->rs", fore_err, other_later, preferred_element_type=jnp.float32
    )
    to_later = jnp.einsum("lrc,cs->lrs", back_err, other_early, preferred_element_type=jnp.float32)
    return (to_early, to_later)


def other_terms(errors, own_views):
    sym_err, fore_err, back_err = errors
    own_early, own_later = own_views
    to_early = jnp.einsum("rc,rs->cs", sym_err, own_early, preferred_element_type=jnp.float32)
    to_early = to_early + jnp.einsum(
        "lrc,lrs->cs", back_err, own_later, preferred_element_type=jnp.float32
    )
    to_later = jnp.einsum("lrc,rs->lcs", fore_err, own_early, preferred_element_type=jnp.float32)
    return (to_early, to_later)


def shards(record, target, offset, lag_steps):
    block_rows = record.shape[0]
    begin_at = offset[0]
    win_width = SAMPLES + SLACK
    window = lax.dynamic_slice_in_dim(record, begin_at, win_width, 1)
    own_views = split_views(window, lag_steps)
    devices = lax.axis_size("region")
    own_index = lax.axis_index("region")
    stacked = target.shape[0]
    received = lax.all_to_all(target, "region", split_axis=2, concat_axis=2, tiled=True)
    flipped = (
        received.reshape(stacked, block_rows, devices, block_rows)
        .transpose(0, 3, 2, 1)
        .reshape(stacked, block_rows, devices * block_rows)
    )
    errors = pair_tiles(
        own_views, own_views, target, flipped, own_index * block_rows, block_rows, 1.0
    )
    grad_early, grad_later = own_terms(errors, own_views)
    halfway = devices // 2

    def visit_block(step_number, loop_state):
        visitor, partials, grad_early, grad_later = loop_state
        visitor = shifted(visitor, "region", 1)
        partials = shifted(partials, "region", 1)
        block_id = (own_index - step_number + devices) % devices
        factor = jnp.where(step_number == halfway, 0.5, 1.0)
        other_views = split_views(visitor, lag_steps)
        errors = pair_tiles(
            own_views, other_views, target, flipped, block_id * block_rows, block_rows, factor
        )
        add_early, add_later = own_terms(errors, other_views)
        to_early, to_later = other_terms(errors, own_views)
        partials = partials + place_views(to_early, to_later, lag_steps, win_width)
        return (visitor, partials, grad_early + add_early, grad_later + add_later)

    def visit_four(turn_number, loop_state):
        for inner in range(4):
            loop_state = visit_block(1 + 4 * turn_number + inner, loop_state)
        return loop_state

    start_state = (window, jnp.zeros((block_rows, win_width), jnp.float32), grad_early, grad_later)
    final_state = lax.fori_loop(0, halfway // 4, visit_four, start_state)
    returned = shifted(final_state[1], "region", halfway)
    in_window = place_views(final_state[2], final_state[3], lag_steps, win_width) + returned
    grad = lax.dynamic_update_slice(jnp.zeros(record.shape, jnp.float32), in_window, (0, begin_at))
    return grad


def solution(mesh):
    placed = (
        P(("groups", "region"), None),
        P(None, ("groups", "region"), None),
        P("groups"),
        P("groups"),
    )
    return jax.shard_map(
        shards, mesh=mesh, in_specs=placed, out_specs=P(("groups", "region"), None), check_vma=False
    )
```

profile of v0, /device:TPU:0, one launch (start us, length us, event | category | flops | bytes accessed | tf_op | source)
XLA Modules:
  0.0 1366.3 jit_solution(1209809443540427602)
XLA Ops:
  0.0 54.7 %copy.41 = bf16[4,512,8192]{1,0,2:T(4,128)(2,1)} copy(bf16[4,512,8192]{2,1,0:T(8,128)(2,1)} %param.7) | data formatting | bytes 67108864 | tf_op args[1]
  54.7 7.6 all-to-all-start
  82.9 568.3 %all-to-all-done = bf16[4,512,8192]{1,0,2:T(4,128)(2,1)} async-done(((bf16[4,512,8192]{1,0,2:T(4,128)(2,1)}), bf16[4,512,8192]{1,0,2:T(4,128)(2,1)}, u32[]{:S(2)}, u32[]{:S(2)}) %all-to-all-start) | async-done | bytes 33554464 | tf_op jit(solution)/shard_map/all_to_all | solution.py:96
  651.2 31.1 %copy.58 = bf16[4,512,16,512]{1,2,3,0:T(8,128)(2,1)} copy(bf16[4,512,16,512]{1,0,3,2:T(4,128)(2,1)} %bitcast.2) | data formatting | bytes 67108864 | tf_op jit(solution)/shard_map/reshape | solution.py:98
  682.3 50.0 %reshape.7 = bf16[4,512,8192]{2,1,0:T(8,128)(2,1)} reshape(bf16[4,512,16,512]{3,2,1,0:T(8,128)(2,1)} %bitcast.439) | data formatting | bytes 67108864 | tf_op jit(solution)/shard_map/reshape | solution.py:100
  742.2 569.7 %while.23 = (s32[]{:T(128)}, bf16[512,512]{1,0:T(8,128)(2,1)S(1)}, f32[512,512]{1,0:T(8,128)}, f32[512,384]{1,0:T(8,128)}, f32[3,512,384]{2,1,0:T(8,128)}, /*ind...) while((s32[]{:T(128)}, bf16[512,512]{1,0:T(8,128)(2,1)S(1)}, ...), condition=%wide.region_1.2_spmd.clone, body=%wide.region_0.1_spmd.clone.sunk | while | flops 16968056832 | bytes 541067456 | solution.py:129
  744.3 44.9 %collective-permute-start.4 = (f32[512,512]{1,0:T(8,128)}, f32[512,512]{1,0:T(8,128)}, u32[]{:S(2)}, u32[]{:S(2)}) collective-permute-start(f32[512,512]{1,0:T(8,128)} %broadcast_select_fusion.2), channel_id=1, source_target_pairs={{0,1},{1,2},{2,3},{3,4},{4,5},{5,6},{6,7},{7,8},{8,9},{9,10},{10,1... | collective-permute-start | bytes 3145736 | tf_op jit(solution)/shard_map/while/body/eval_jaxpr/ppermute | solution.py:15
  789.2 15.5 %dynamic-slice_convert_fusion.11 = (f32[4,512,512]{2,1,0:T(8,128)}, f32[4,512,512]{2,1,0:T(8,128)}, f32[4,512,512]{2,1,0:T(8,128)}, f32[4,512,512]{2,1,0:T(8,128...) fusion(bf16[4,512,8192]{2,1,0:T(8,128)(2,1)} %get-tuple-element, ...), kind=kLoop, calls=%fused_computation.25.clone.1 | loop fusion | flops 8388608 | bytes 50331664 | tf_op jit(solution)/shard_map/while/body/eval_jaxpr/convert_element_type | solution.py:49
  804.7 80.8 %collective-permute-done = bf16[512,512]{1,0:T(8,128)(2,1)S(1)} collective-permute-done((bf16[512,512]{1,0:T(8,128)(2,1)S(1)}, bf16[512,512]{1,0:T(8,128)(2,1)S(1)}, u32[]{:S(2)}, u32[]{:S(2)}) %collective-permute-start) | collective-permute-done | bytes 524320 | tf_op jit(solution)/shard_map/while/body/eval_jaxpr/ppermute | solution.py:15
  936.7 11.3 collective-permute-done.1
  988.1 5.9 collective-permute-done.2
  1006.4 5.2 add.913
  1014.2 5.2 add.914
  1022.1 5.2 add.915
  1048.9 6.5 add.917
  1057.7 6.5 add.918
  1072.5 6.5 add.919
  1082.0 6.1 add_add_fusion.2
  1093.6 15.5 %dynamic-slice_convert_fusion.11 = (f32[4,512,512]{2,1,0:T(8,128)}, f32[4,512,512]{2,1,0:T(8,128)}, f32[4,512,512]{2,1,0:T(8,128)}, f32[4,512,512]{2,1,0:T(8,128...) fusion(bf16[4,512,8192]{2,1,0:T(8,128)(2,1)} %get-tuple-element, ...), kind=kLoop, calls=%fused_computation.25.clone.1 | loop fusion | flops 8388608 | bytes 50331664 | tf_op jit(solution)/shard_map/while/body/eval_jaxpr/convert_element_type | solution.py:49
  1160.4 6.0 collective-permute-done.1
  1206.0 6.1 collective-permute-done.2
  1224.5 5.2 add.913
  1240.2 5.2 add.915
  1267.0 6.5 add.917
  1275.8 6.5 add.918
  1290.6 6.5 add.919
  1300.1 6.1 add_add_fusion.2
  1314.8 6.9 add.709
  1323.1 6.9 add.711
  1331.4 6.9 add.713
  1338.3 18.9 %collective-permute-done.8 = f32[512,512]{1,0:T(8,128)} collective-permute-done((f32[512,512]{1,0:T(8,128)}, f32[512,512]{1,0:T(8,128)}, u32[]{:S(2)}, u32[]{:S(2)}) %collective-permute-start.8) | collective-permute-done | bytes 1048608 | tf_op jit(solution)/shard_map/ppermute | solution.py:15
  1359.8 6.1 dynamic_update_slice.75
  (306 shorter events, 334.3 us)
Async XLA Ops:
  54.7 7.6 copy-start.34
  54.7 14.5 %copy-start.32 = (bf16[512,640]{1,0:T(8,128)(2,1)S(1)}, bf16[512,640]{1,0:T(8,128)(2,1)}, u32[]{:S(2)}) copy-start(bf16[512,640]{1,0:T(8,128)(2,1)} %param.6) | copy-start | bytes 1966084
  54.7 596.5 %all-to-all-start = ((bf16[4,512,8192]{1,0,2:T(4,128)(2,1)}), bf16[4,512,8192]{1,0,2:T(4,128)(2,1)}, u32[]{:S(2)}, u32[]{:S(2)}) async-start(bf16[4,512,8192]{1,0,2:T(4,128)(2,1)} %copy.41), calls=%async_computation | async-start | bytes 67108864 | tf_op jit(solution)/shard_map/all_to_all | solution.py:96
  76.6 4.3 copy-start.25
  732.2 4.4 copy-start.27
  742.4 143.1 %collective-permute-start = (bf16[512,512]{1,0:T(8,128)(2,1)S(1)}, bf16[512,512]{1,0:T(8,128)(2,1)S(1)}, u32[]{:S(2)}, u32[]{:S(2)}) collective-permute-start(bf16[512,512]{1,0:T(8,128)(2,1)S(1)} %get-tuple-element.604), channel_id=1, source_target_pairs={{0,1},{1,2},{2,3},{3,4},{4,5},{5,6},{6,7},{7,8},{8,9},{9,10},{10,1... | collective-permute-start | bytes 1572872 | tf_op jit(solution)/shard_map/while/body/eval_jaxpr/ppermute | solution.py:15
  744.3 208.1 %collective-permute-start.4 = (f32[512,512]{1,0:T(8,128)}, f32[512,512]{1,0:T(8,128)}, u32[]{:S(2)}, u32[]{:S(2)}) collective-permute-start(f32[512,512]{1,0:T(8,128)} %broadcast_select_fusion.2), channel_id=1, source_target_pairs={{0,1},{1,2},{2,3},{3,4},{4,5},{5,6},{6,7},{7,8},{8,9},{9,10},{10,1... | collective-permute-start | bytes 3145736 | tf_op jit(solution)/shard_map/while/body/eval_jaxpr/ppermute | solution.py:15
  931.1 16.8 %collective-permute-start.1 = (bf16[512,512]{1,0:T(8,128)(2,1)S(1)}, bf16[512,512]{1,0:T(8,128)(2,1)S(1)}, u32[]{:S(2)}, u32[]{:S(2)}) collective-permute-start(bf16[512,512]{1,0:T(8,128)(2,1)S(1)} %collective-permute-done), channel_id=1, source_target_pairs={{0,1},{1,2},{2,3},{3,4},{4,5},{5,6},{6,7},{7,8},{8,9},{9,10},{10,1... | collective-permute-start | bytes 1572872 | tf_op jit(solution)/shard_map/while/body/eval_jaxpr/ppermute | solution.py:15
  934.2 14.2 %copy-start.11 = (f32[4,512,512]{2,1,0:T(8,128)S(1)}, f32[4,512,512]{2,1,0:T(8,128)}, u32[]{:S(2)}) copy-start(f32[4,512,512]{2,1,0:T(8,128)} %get-tuple-element.562) | copy-start | bytes 12582916 | tf_op jit(solution)/shard_map/while
  951.4 4.5 copy-start.2
  952.4 7.7 copy-start.5
  955.9 77.9 %collective-permute-start.5 = (f32[512,512]{1,0:T(8,128)}, f32[512,512]{1,0:T(8,128)}, u32[]{:S(2)}, u32[]{:S(2)}) collective-permute-start(f32[512,512]{1,0:T(8,128)} %add.908), channel_id=1, source_target_pairs={{0,1},{1,2},{2,3},{3,4},{4,5},{5,6},{6,7},{7,8},{8,9},{9,10},{10,1... | collective-permute-start | bytes 3145736 | tf_op jit(solution)/shard_map/while/body/eval_jaxpr/ppermute | solution.py:15
  982.2 11.7 collective-permute-start.2
  985.7 8.3 copy-start.1
  1027.3 11.3 collective-permute-start.3
  1031.4 7.2 copy-start
  1036.5 31.3 %collective-permute-start.6 = (f32[512,512]{1,0:T(8,128)}, f32[512,512]{1,0:T(8,128)}, u32[]{:S(2)}, u32[]{:S(2)}) collective-permute-start(f32[512,512]{1,0:T(8,128)} %add.912), channel_id=1, source_target_pairs={{0,1},{1,2},{2,3},{3,4},{4,5},{5,6},{6,7},{7,8},{8,9},{9,10},{10,1... | collective-permute-start | bytes 3145736 | tf_op jit(solution)/shard_map/while/body/eval_jaxpr/ppermute | solution.py:15
  1070.2 17.9 %collective-permute-start.7 = (f32[512,512]{1,0:T(8,128)}, f32[512,512]{1,0:T(8,128)}, u32[]{:S(2)}, u32[]{:S(2)}) collective-permute-start(f32[512,512]{1,0:T(8,128)} %add.916), channel_id=1, source_target_pairs={{0,1},{1,2},{2,3},{3,4},{4,5},{5,6},{6,7},{7,8},{8,9},{9,10},{10,1... | collective-permute-start | bytes 3145736 | tf_op jit(solution)/shard_map/while/body/eval_jaxpr/ppermute | solution.py:15
  1090.7 18.3 %collective-permute-start = (bf16[512,512]{1,0:T(8,128)(2,1)S(1)}, bf16[512,512]{1,0:T(8,128)(2,1)S(1)}, u32[]{:S(2)}, u32[]{:S(2)}) collective-permute-start(bf16[512,512]{1,0:T(8,128)(2,1)S(1)} %get-tuple-element.604), channel_id=1, source_target_pairs={{0,1},{1,2},{2,3},{3,4},{4,5},{5,6},{6,7},{7,8},{8,9},{9,10},{10,1... | collective-permute-start | bytes 1572872 | tf_op jit(solution)/shard_map/while/body/eval_jaxpr/ppermute | solution.py:15
  1093.5 77.4 %collective-permute-start.4 = (f32[512,512]{1,0:T(8,128)}, f32[512,512]{1,0:T(8,128)}, u32[]{:S(2)}, u32[]{:S(2)}) collective-permute-start(f32[512,512]{1,0:T(8,128)} %broadcast_select_fusion.2), channel_id=1, source_target_pairs={{0,1},{1,2},{2,3},{3,4},{4,5},{5,6},{6,7},{7,8},{8,9},{9,10},{10,1... | collective-permute-start | bytes 3145736 | tf_op jit(solution)/shard_map/while/body/eval_jaxpr/ppermute | solution.py:15
  1154.7 11.7 collective-permute-start.1
  1158.0 8.9 copy-start.11
  1169.9 4.5 copy-start.2
  1170.9 7.7 copy-start.5
  1174.4 77.6 %collective-permute-start.5 = (f32[512,512]{1,0:T(8,128)}, f32[512,512]{1,0:T(8,128)}, u32[]{:S(2)}, u32[]{:S(2)}) collective-permute-start(f32[512,512]{1,0:T(8,128)} %add.908), channel_id=1, source_target_pairs={{0,1},{1,2},{2,3},{3,4},{4,5},{5,6},{6,7},{7,8},{8,9},{9,10},{10,1... | collective-permute-start | bytes 3145736 | tf_op jit(solution)/shard_map/while/body/eval_jaxpr/ppermute | solution.py:15
  1200.6 11.5 collective-permute-start.2
  1203.7 8.4 copy-start.1
  1245.5 11.3 collective-permute-start.3
  1249.5 7.2 copy-start
  1254.7 31.3 %collective-permute-start.6 = (f32[512,512]{1,0:T(8,128)}, f32[512,512]{1,0:T(8,128)}, u32[]{:S(2)}, u32[]{:S(2)}) collective-permute-start(f32[512,512]{1,0:T(8,128)} %add.912), channel_id=1, source_target_pairs={{0,1},{1,2},{2,3},{3,4},{4,5},{5,6},{6,7},{7,8},{8,9},{9,10},{10,1... | collective-permute-start | bytes 3145736 | tf_op jit(solution)/shard_map/while/body/eval_jaxpr/ppermute | solution.py:15
  1288.3 17.9 %collective-permute-start.7 = (f32[512,512]{1,0:T(8,128)}, f32[512,512]{1,0:T(8,128)}, u32[]{:S(2)}, u32[]{:S(2)}) collective-permute-start(f32[512,512]{1,0:T(8,128)} %add.916), channel_id=1, source_target_pairs={{0,1},{1,2},{2,3},{3,4},{4,5},{5,6},{6,7},{7,8},{8,9},{9,10},{10,1... | collective-permute-start | bytes 3145736 | tf_op jit(solution)/shard_map/while/body/eval_jaxpr/ppermute | solution.py:15
  1312.0 45.2 %collective-permute-start.8 = (f32[512,512]{1,0:T(8,128)}, f32[512,512]{1,0:T(8,128)}, u32[]{:S(2)}, u32[]{:S(2)}) collective-permute-start(f32[512,512]{1,0:T(8,128)} %get-tuple-element.357), channel_id=1, source_target_pairs={{0,8},{1,9},{2,10},{3,11},{4,12},{5,13},{6,14},{7,15},{8,0},{9,1},... | collective-permute-start | bytes 3145736 | tf_op jit(solution)/shard_map/ppermute | solution.py:15
  (48 other events, 102.5 us)
where the time goes:
time: 1380 us; the launch traced here: 1370 us
  waiting for transfers between devices  701 us (51%)
  local copies, waits for them, and re-layouts  341 us (25%)
  matrix products  130 us (9%)
  other arithmetic  127 us (9%)
  starting transfers between devices  55.9 us (4%)
    all_to_all x1, waiting for transfers between devices, shards(): lax.all_to_all(target, 'region', split_axis=2, concat_axis=2, tiled=True)  568 us
    add x27, local copies, waits for them, and re-layouts, place_views(): placed + lax.dynamic_update_slice(blank, later_parts[lag_number], (0, lag...  153 us
    ppermute x17, waiting for transfers between devices, shifted(): return lax.ppermute(value, axis, pairs)  133 us
    unnamed x17, local copies, waits for them, and re-layouts  58.8 us
    dynamic_update_slice x27, other arithmetic, place_views(): lax.dynamic_update_slice(blank, later_parts[lag_number], (0, lag_steps[la...  56.8 us
    reshape x1, local copies, waits for them, and re-layouts, shards(): flipped = received.reshape(stacked, block_rows, devices, block_rows).tran...  50 us
    ppermute x17, starting transfers between devices, shifted(): return lax.ppermute(value, axis, pairs)  48.3 us
    convert_element_type x3, other arithmetic, pair_tiles(): lax.dynamic_slice_in_dim(flipped, column_at, width, 2).astype(jnp.float32)  33.3 us
  transfers between devices with their start and end apart: 18, of which 9 were waited for; matrix products, arithmetic and copies ran while one was open for 30% of the time, Pallas kernels for 0%

commit v1 on v0

--- a/solution.py
+++ b/solution.py
@@ -93,7 +93,26 @@
     devices = lax.axis_size("region")
     own_index = lax.axis_index("region")
     stacked = target.shape[0]
-    received = lax.all_to_all(target, "region", split_axis=2, concat_axis=2, tiled=True)
+
+    def trace_marks_up(tile_in):
+        net_axis = "region"
+        local_now = lax.axis_index(net_axis)
+        main = lax.axis_size(net_axis)
+        z, y_new = (main, local_now)
+        moved = tile_in.shape[2] // z
+        b_next = list(tile_in.shape)
+        b_next[2] = moved
+        a_now = b_next[2]
+        b_next[2] = a_now * z
+        w2 = jnp.zeros(b_next, tile_in.dtype)
+        for j in tuple(range(z)):
+            then = lax.dynamic_slice_in_dim(tile_in, (y_new ^ j) * moved, moved, axis=2)
+            if j:
+                then = lax.ppermute(then, net_axis, [(q, q ^ j) for q in range(z)])
+            w2 = lax.dynamic_update_slice_in_dim(w2, then, (y_new ^ j) * a_now, axis=2)
+        return w2
+
+    received = trace_marks_up(target)
     flipped = (
         received.reshape(stacked, block_rows, devices, block_rows)
         .transpose(0, 3, 2, 1)

time: 1380 us -> 1460 us (1.058)
  starting transfers between devices: 55.9 us -> 249 us
  waiting for transfers between devices: 701 us -> 559 us
  other arithmetic: 127 us -> 144 us
    all_to_all x1 -> x0, waiting for transfers between devices: 568 us -> none  [shards(): lax.all_to_all(target, 'region', split_axis=2, concat_axis=2, tiled=True)]
    ppermute x0 -> x15, waiting for transfers between devices: none -> 501 us  [trace_marks_up(): then = lax.ppermute(then, net_axis, [(q, q ^ j) for q in range(z)])]
    ppermute x17, starting transfers between devices: 48.3 us -> 224 us  [shifted(): return lax.ppermute(value, axis, pairs)]
    ppermute x17, waiting for transfers between devices: 133 us -> 57.7 us  [shifted(): return lax.ppermute(value, axis, pairs)]
    dynamic_update_slice x0 -> x16, local copies, waits for them, and re-layouts: none -> 40.5 us  [trace_marks_up(): w2 = lax.dynamic_update_slice_in_dim(w2, then, (y_new ^ j) * a_now, axis=2)]
    reshape x1 -> x0, local copies, waits for them, and re-layouts: 31.1 us -> none  [shards(): received.reshape(stacked, block_rows, devices, block_rows)]
    reshape x1, local copies, waits for them, and re-layouts: 50 us -> 22.7 us  [shards(): flipped = received.reshape(stacked, block_rows, devices, block_rows).tran...]
    ppermute x0 -> x15, starting transfers between devices: none -> 24.7 us  [trace_marks_up(): then = lax.ppermute(then, net_axis, [(q, q ^ j) for q in range(z)])]
  transfers between devices with their start and end apart: 18 -> 32, of which waited for: 9 -> 13; matrix products, arithmetic and copies ran while one was open for 30% -> 36% of each run, Pallas kernels for 0% -> 0%
where the time goes in v1:
time: 1460 us; the launch traced here: 1450 us
  waiting for transfers between devices  559 us (38%)
  local copies, waits for them, and re-layouts  352 us (24%)
  starting transfers between devices  249 us (17%)
  other arithmetic  144 us (10%)
  matrix products  134 us (9%)
    ppermute x15, waiting for transfers between devices, trace_marks_up(): then = lax.ppermute(then, net_axis, [(q, q ^ j) for q in range(z)])  501 us
    ppermute x17, starting transfers between devices, shifted(): return lax.ppermute(value, axis, pairs)  224 us
    add x27, local copies, waits for them, and re-layouts, place_views(): placed + lax.dynamic_update_slice(blank, later_parts[lag_number], (0, lag...  161 us
    unnamed x37, local copies, waits for them, and re-layouts  65.5 us
    ppermute x17, waiting for transfers between devices, shifted(): return lax.ppermute(value, axis, pairs)  57.7 us
    dynamic_update_slice x27, other arithmetic, place_views(): lax.dynamic_update_slice(blank, later_parts[lag_number], (0, lag_steps[la...  55.1 us
    dynamic_update_slice x16, local copies, waits for them, and re-layouts, trace_marks_up(): w2 = lax.dynamic_update_slice_in_dim(w2, then, (y_new ^ j) * a_now, axis=2)  40.5 us
    convert_element_type x3, other arithmetic, pair_tiles(): lax.dynamic_slice_in_dim(flipped, column_at, width, 2).astype(jnp.float32)  33.3 us
  transfers between devices with their start and end apart: 32, of which 13 were waited for; matrix products, arithmetic and copies ran while one was open for 36% of the time, Pallas kernels for 0%

profile of v1, /device:TPU:0, one launch (start us, length us, event | category | flops | bytes accessed | tf_op | source)
XLA Modules:
  0.0 1449.0 jit_solution(10780023558870916601)
XLA Ops:
  0.0 24.2 %constant_dynamic-slice_fusion.1 = (bf16[4,512,512]{2,1,0:T(8,128)(2,1)}, bf16[4,512,512]{2,1,0:T(8,128)(2,1)}, bf16[4,512,512]{2,1,0:T(8,128)(2,1)}, bf16[4,512...) fusion(bf16[4,512,8192]{2,1,0:T(8,128)(2,1)} %param.7, ...), kind=kLoop, calls=%fused_computation.204 | loop fusion | flops 1048576 | bytes 71303232 | tf_op jit(solution)/shard_map/dynamic_slice | solution.py:109
  60.9 21.5 %collective-permute-done.9 = bf16[4,512,512]{1,2,0:T(8,128)(2,1)} collective-permute-done((bf16[4,512,512]{1,2,0:T(8,128)(2,1)}, bf16[4,512,512]{1,2,0:T(8,128)(2,1)}, u32[]{:S(2)}, u32[]{:S(2)}) %collective-permute-start.9) | collective-permute-done | bytes 2097184 | tf_op jit(solution)/shard_map/ppermute | solution.py:111
  88.4 38.5 %collective-permute-done.10 = bf16[4,512,512]{1,2,0:T(8,128)(2,1)} collective-permute-done((bf16[4,512,512]{1,2,0:T(8,128)(2,1)}, bf16[4,512,512]{1,2,0:T(8,128)(2,1)}, u32[]{:S(2)}, u32[]{:S(2)}) %collective-permute-start.10) | collective-permute-done | bytes 2097184 | tf_op jit(solution)/shard_map/ppermute | solution.py:111
  138.0 88.5 %collective-permute-done.12 = bf16[4,512,512]{1,2,0:T(8,128)(2,1)} collective-permute-done((bf16[4,512,512]{1,2,0:T(8,128)(2,1)}, bf16[4,512,512]{1,2,0:T(8,128)(2,1)}, u32[]{:S(2)}, u32[]{:S(2)}) %collective-permute-start.12) | collective-permute-done | bytes 2097184 | tf_op jit(solution)/shard_map/ppermute | solution.py:111
  248.9 25.0 %collective-permute-done.13 = bf16[4,512,512]{1,2,0:T(8,128)(2,1)} collective-permute-done((bf16[4,512,512]{1,2,0:T(8,128)(2,1)}, bf16[4,512,512]{1,2,0:T(8,128)(2,1)}, u32[]{:S(2)}, u32[]{:S(2)}) %collective-permute-start.13) | collective-permute-done | bytes 2097184 | tf_op jit(solution)/shard_map/ppermute | solution.py:111
  299.7 17.8 %collective-permute-done.14 = bf16[4,512,512]{1,2,0:T(8,128)(2,1)} collective-permute-done((bf16[4,512,512]{1,2,0:T(8,128)(2,1)}, bf16[4,512,512]{1,2,0:T(8,128)(2,1)}, u32[]{:S(2)}, u32[]{:S(2)}) %collective-permute-start.14) | collective-permute-done | bytes 2097184 | tf_op jit(solution)/shard_map/ppermute | solution.py:111
  321.1 11.0 broadcast_in_dim.7
  341.7 248.0 %collective-permute-done.17 = bf16[4,512,512]{1,2,0:T(8,128)(2,1)} collective-permute-done((bf16[4,512,512]{1,2,0:T(8,128)(2,1)}, bf16[4,512,512]{1,2,0:T(8,128)(2,1)}, u32[]{:S(2)}, u32[]{:S(2)}) %collective-permute-start.17) | collective-permute-done | bytes 2097184 | tf_op jit(solution)/shard_map/ppermute | solution.py:111
  617.9 61.7 %collective-permute-done.18 = bf16[4,512,512]{1,2,0:T(8,128)(2,1)} collective-permute-done((bf16[4,512,512]{1,2,0:T(8,128)(2,1)}, bf16[4,512,512]{1,2,0:T(8,128)(2,1)}, u32[]{:S(2)}, u32[]{:S(2)}) %collective-permute-start.18) | collective-permute-done | bytes 2097184 | tf_op jit(solution)/shard_map/ppermute | solution.py:111
  688.3 22.7 %copy.86 = bf16[4,16,64,8,512]{4,3,1,2,0:T(8,128)(2,1)} copy(bf16[4,16,64,8,512]{4,3,2,1,0:T(8,128)(2,1)} %bitcast.440) | data formatting | bytes 67108864 | tf_op jit(solution)/shard_map/reshape | solution.py:119
  720.9 677.1 %while.23 = (s32[]{:T(128)}, bf16[512,512]{1,0:T(8,128)(2,1)S(1)}, f32[512,512]{1,0:T(8,128)}, f32[512,384]{1,0:T(8,128)}, f32[3,512,384]{2,1,0:T(8,128)}, /*ind...) while((s32[]{:T(128)}, bf16[512,512]{1,0:T(8,128)(2,1)S(1)}, ...), condition=%wide.region_1.2_spmd.clone, body=%wide.region_0.1_spmd.clone.sunk | while | flops 16968056832 | bytes 553650496 | solution.py:148
  722.7 15.5 %dynamic-slice_convert_fusion.10 = (f32[4,512,512]{2,1,0:T(8,128)}, f32[4,512,512]{2,1,0:T(8,128)}, f32[4,512,512]{2,1,0:T(8,128)}, f32[4,512,512]{2,1,0:T(8,128...) fusion(bf16[4,512,8192]{2,1,0:T(8,128)(2,1)} %get-tuple-element, ...), kind=kLoop, calls=%fused_computation.25.clone.1 | loop fusion | flops 8388608 | bytes 50331664 | tf_op jit(solution)/shard_map/while/body/eval_jaxpr/convert_element_type | solution.py:49
  804.7 6.5 add.986
  813.5 6.5 add.987
  822.3 6.5 add.988
  834.4 202.3 %collective-permute-start.5 = (f32[512,512]{1,0:T(8,128)}, f32[512,512]{1,0:T(8,128)}, u32[]{:S(2)}, u32[]{:S(2)}) collective-permute-start(f32[512,512]{1,0:T(8,128)} %add.985), channel_id=1, source_target_pairs={{0,1},{1,2},{2,3},{3,4},{4,5},{5,6},{6,7},{7,8},{8,9},{9,10},{10,1... | collective-permute-start | bytes 3145736 | tf_op jit(solution)/shard_map/while/body/eval_jaxpr/ppermute | solution.py:15
  1081.0 8.4 collective-permute-start.3
  1111.6 6.5 add.994
  1120.3 6.5 add.995
  1137.6 6.5 add.996
  1161.0 15.5 %dynamic-slice_convert_fusion.10 = (f32[4,512,512]{2,1,0:T(8,128)}, f32[4,512,512]{2,1,0:T(8,128)}, f32[4,512,512]{2,1,0:T(8,128)}, f32[4,512,512]{2,1,0:T(8,128...) fusion(bf16[4,512,8192]{2,1,0:T(8,128)(2,1)} %get-tuple-element, ...), kind=kLoop, calls=%fused_computation.25.clone.1 | loop fusion | flops 8388608 | bytes 50331664 | tf_op jit(solution)/shard_map/while/body/eval_jaxpr/convert_element_type | solution.py:49
  1243.1 6.5 add.986
  1251.9 6.5 add.987
  1260.7 6.5 add.988
  1276.8 18.8 %collective-permute-done.2 = bf16[512,512]{1,0:T(8,128)(2,1)S(1)} collective-permute-done((bf16[512,512]{1,0:T(8,128)(2,1)S(1)}, bf16[512,512]{1,0:T(8,128)(2,1)S(1)}, u32[]{:S(2)}, u32[]{:S(2)}) %collective-permute-start.2) | collective-permute-done | bytes 524320 | tf_op jit(solution)/shard_map/while/body/eval_jaxpr/ppermute | solution.py:15
  1353.1 6.5 add.994
  1361.9 6.5 add.995
  1376.7 6.5 add.996
  1400.9 6.9 add.786
  1409.2 6.9 add.788
  1417.5 6.9 add.790
  1424.4 15.5 %collective-permute-done.23 = f32[512,512]{1,0:T(8,128)} collective-permute-done((f32[512,512]{1,0:T(8,128)}, f32[512,512]{1,0:T(8,128)}, u32[]{:S(2)}, u32[]{:S(2)}) %collective-permute-start.23) | collective-permute-done | bytes 1048608 | tf_op jit(solution)/shard_map/ppermute | solution.py:15
  (387 shorter events, 503.9 us)
Async XLA Ops:
  28.4 25.8 %collective-permute-start.8 = (bf16[4,512,512]{1,2,0:T(8,128)(2,1)}, bf16[4,512,512]{1,2,0:T(8,128)(2,1)}, u32[]{:S(2)}, u32[]{:S(2)}) collective-permute-start(bf16[4,512,512]{1,2,0:T(8,128)(2,1)} %copy.71), channel_id=1, source_target_pairs={{0,1},{1,0},{2,3},{3,2},{4,5},{5,4},{6,7},{7,6},{8,9},{9,8},{10,11... | collective-permute-start | bytes 6291464 | tf_op jit(solution)/shard_map/ppermute | solution.py:111
  33.0 49.3 %collective-permute-start.9 = (bf16[4,512,512]{1,2,0:T(8,128)(2,1)}, bf16[4,512,512]{1,2,0:T(8,128)(2,1)}, u32[]{:S(2)}, u32[]{:S(2)}) collective-permute-start(bf16[4,512,512]{1,2,0:T(8,128)(2,1)} %copy.72), channel_id=1, source_target_pairs={{0,2},{1,3},{2,0},{3,1},{4,6},{5,7},{6,4},{7,5},{8,10},{9,11},{10,... | collective-permute-start | bytes 6291464 | tf_op jit(solution)/shard_map/ppermute | solution.py:111
  39.7 87.2 %collective-permute-start.10 = (bf16[4,512,512]{1,2,0:T(8,128)(2,1)}, bf16[4,512,512]{1,2,0:T(8,128)(2,1)}, u32[]{:S(2)}, u32[]{:S(2)}) collective-permute-start(bf16[4,512,512]{1,2,0:T(8,128)(2,1)} %copy.73), channel_id=1, source_target_pairs={{0,3},{1,2},{2,1},{3,0},{4,7},{5,6},{6,5},{7,4},{8,11},{9,10},{10,... | collective-permute-start | bytes 6291464 | tf_op jit(solution)/shard_map/ppermute | solution.py:111
  44.0 89.7 %collective-permute-start.11 = (bf16[4,512,512]{1,2,0:T(8,128)(2,1)}, bf16[4,512,512]{1,2,0:T(8,128)(2,1)}, u32[]{:S(2)}, u32[]{:S(2)}) collective-permute-start(bf16[4,512,512]{1,2,0:T(8,128)(2,1)} %copy.74), channel_id=1, source_target_pairs={{0,4},{1,5},{2,6},{3,7},{4,0},{5,1},{6,2},{7,3},{8,12},{9,13},{10,... | collective-permute-start | bytes 6291464 | tf_op jit(solution)/shard_map/ppermute | solution.py:111
  50.0 176.5 %collective-permute-start.12 = (bf16[4,512,512]{1,2,0:T(8,128)(2,1)}, bf16[4,512,512]{1,2,0:T(8,128)(2,1)}, u32[]{:S(2)}, u32[]{:S(2)}) collective-permute-start(bf16[4,512,512]{1,2,0:T(8,128)(2,1)} %copy.75), channel_id=1, source_target_pairs={{0,5},{1,4},{2,7},{3,6},{4,1},{5,0},{6,3},{7,2},{8,13},{9,12},{10,... | collective-permute-start | bytes 6291464 | tf_op jit(solution)/shard_map/ppermute | solution.py:111
  54.1 219.7 %collective-permute-start.13 = (bf16[4,512,512]{1,2,0:T(8,128)(2,1)}, bf16[4,512,512]{1,2,0:T(8,128)(2,1)}, u32[]{:S(2)}, u32[]{:S(2)}) collective-permute-start(bf16[4,512,512]{1,2,0:T(8,128)(2,1)} %copy.76), channel_id=1, source_target_pairs={{0,6},{1,7},{2,4},{3,5},{4,2},{5,3},{6,0},{7,1},{8,14},{9,15},{10,... | collective-permute-start | bytes 6291464 | tf_op jit(solution)/shard_map/ppermute | solution.py:111
  82.3 235.2 %collective-permute-start.14 = (bf16[4,512,512]{1,2,0:T(8,128)(2,1)}, bf16[4,512,512]{1,2,0:T(8,128)(2,1)}, u32[]{:S(2)}, u32[]{:S(2)}) collective-permute-start(bf16[4,512,512]{1,2,0:T(8,128)(2,1)} %copy.77), channel_id=1, source_target_pairs={{0,7},{1,6},{2,5},{3,4},{4,3},{5,2},{6,1},{7,0},{8,15},{9,14},{10,... | collective-permute-start | bytes 6291464 | tf_op jit(solution)/shard_map/ppermute | solution.py:111
  126.9 206.6 %collective-permute-start.15 = (bf16[4,512,512]{1,2,0:T(8,128)(2,1)}, bf16[4,512,512]{1,2,0:T(8,128)(2,1)}, u32[]{:S(2)}, u32[]{:S(2)}) collective-permute-start(bf16[4,512,512]{1,2,0:T(8,128)(2,1)} %copy.78), channel_id=1, source_target_pairs={{0,8},{1,9},{2,10},{3,11},{4,12},{5,13},{6,14},{7,15},{8,0},{9,1},... | collective-permute-start | bytes 6291464 | tf_op jit(solution)/shard_map/ppermute | solution.py:111
  133.7 201.4 %collective-permute-start.16 = (bf16[4,512,512]{1,2,0:T(8,128)(2,1)}, bf16[4,512,512]{1,2,0:T(8,128)(2,1)}, u32[]{:S(2)}, u32[]{:S(2)}) collective-permute-start(bf16[4,512,512]{1,2,0:T(8,128)(2,1)} %copy.79), channel_id=1, source_target_pairs={{0,9},{1,8},{2,11},{3,10},{4,13},{5,12},{6,15},{7,14},{8,1},{9,0},... | collective-permute-start | bytes 6291464 | tf_op jit(solution)/shard_map/ppermute | solution.py:111
  226.5 363.3 %collective-permute-start.17 = (bf16[4,512,512]{1,2,0:T(8,128)(2,1)}, bf16[4,512,512]{1,2,0:T(8,128)(2,1)}, u32[]{:S(2)}, u32[]{:S(2)}) collective-permute-start(bf16[4,512,512]{1,2,0:T(8,128)(2,1)} %copy.80), channel_id=1, source_target_pairs={{0,10},{1,11},{2,8},{3,9},{4,14},{5,15},{6,12},{7,13},{8,2},{9,3},... | collective-permute-start | bytes 6291464 | tf_op jit(solution)/shard_map/ppermute | solution.py:111
  273.9 405.7 %collective-permute-start.18 = (bf16[4,512,512]{1,2,0:T(8,128)(2,1)}, bf16[4,512,512]{1,2,0:T(8,128)(2,1)}, u32[]{:S(2)}, u32[]{:S(2)}) collective-permute-start(bf16[4,512,512]{1,2,0:T(8,128)(2,1)} %copy.81), channel_id=1, source_target_pairs={{0,11},{1,10},{2,9},{3,8},{4,15},{5,14},{6,13},{7,12},{8,3},{9,2},... | collective-permute-start | bytes 6291464 | tf_op jit(solution)/shard_map/ppermute | solution.py:111
  317.5 365.1 %collective-permute-start.19 = (bf16[4,512,512]{1,2,0:T(8,128)(2,1)S(1)}, bf16[4,512,512]{1,2,0:T(8,128)(2,1)S(1)}, u32[]{:S(2)}, u32[]{:S(2)}) collective-permute-start(bf16[4,512,512]{1,2,0:T(8,128)(2,1)S(1)} %copy-done.40), channel_id=1, source_target_pairs={{0,12},{1,13},{2,14},{3,15},{4,8},{5,9},{6,10},{7,11},{8,4},{9,5},... | collective-permute-start | bytes 6291464 | tf_op jit(solution)/shard_map/ppermute | solution.py:111
  334.4 349.6 %collective-permute-start.20 = (bf16[4,512,512]{1,2,0:T(8,128)(2,1)S(1)}, bf16[4,512,512]{1,2,0:T(8,128)(2,1)S(1)}, u32[]{:S(2)}, u32[]{:S(2)}) collective-permute-start(bf16[4,512,512]{1,2,0:T(8,128)(2,1)S(1)} %copy-done.39), channel_id=1, source_target_pairs={{0,13},{1,12},{2,15},{3,14},{4,9},{5,8},{6,11},{7,10},{8,5},{9,4},... | collective-permute-start | bytes 6291464 | tf_op jit(solution)/shard_map/ppermute | solution.py:111
  335.1 350.4 %collective-permute-start.21 = (bf16[4,512,512]{1,2,0:T(8,128)(2,1)S(1)}, bf16[4,512,512]{1,2,0:T(8,128)(2,1)S(1)}, u32[]{:S(2)}, u32[]{:S(2)}) collective-permute-start(bf16[4,512,512]{1,2,0:T(8,128)(2,1)S(1)} %copy-done.38), channel_id=1, source_target_pairs={{0,14},{1,15},{2,12},{3,13},{4,10},{5,11},{6,8},{7,9},{8,6},{9,7},... | collective-permute-start | bytes 6291464 | tf_op jit(solution)/shard_map/ppermute | solution.py:111
  589.7 97.2 %collective-permute-start.22 = (bf16[4,512,512]{1,2,0:T(8,128)(2,1)S(1)}, bf16[4,512,512]{1,2,0:T(8,128)(2,1)S(1)}, u32[]{:S(2)}, u32[]{:S(2)}) collective-permute-start(bf16[4,512,512]{1,2,0:T(8,128)(2,1)S(1)} %copy-done.37), channel_id=1, source_target_pairs={{0,15},{1,14},{2,13},{3,12},{4,11},{5,10},{6,9},{7,8},{8,7},{9,6},... | collective-permute-start | bytes 6291464 | tf_op jit(solution)/shard_map/ppermute | solution.py:111
  720.9 17.3 %collective-permute-start = (bf16[512,512]{1,0:T(8,128)(2,1)S(1)}, bf16[512,512]{1,0:T(8,128)(2,1)S(1)}, u32[]{:S(2)}, u32[]{:S(2)}) collective-permute-start(bf16[512,512]{1,0:T(8,128)(2,1)S(1)} %get-tuple-element.623), channel_id=1, source_target_pairs={{0,1},{1,2},{2,3},{3,4},{4,5},{5,6},{6,7},{7,8},{8,9},{9,10},{10,1... | collective-permute-start | bytes 1572872 | tf_op jit(solution)/shard_map/while/body/eval_jaxpr/ppermute | solution.py:15
  722.1 109.7 %collective-permute-start.4 = (f32[512,512]{1,0:T(8,128)}, f32[512,512]{1,0:T(8,128)}, u32[]{:S(2)}, u32[]{:S(2)}) collective-permute-start(f32[512,512]{1,0:T(8,128)} %broadcast_select_fusion.2), channel_id=1, source_target_pairs={{0,1},{1,2},{2,3},{3,4},{4,5},{5,6},{6,7},{7,8},{8,9},{9,10},{10,1... | collective-permute-start | bytes 3145736 | tf_op jit(solution)/shard_map/while/body/eval_jaxpr/ppermute | solution.py:15
  784.0 11.6 collective-permute-start.1
  834.4 265.7 %collective-permute-start.5 = (f32[512,512]{1,0:T(8,128)}, f32[512,512]{1,0:T(8,128)}, u32[]{:S(2)}, u32[]{:S(2)}) collective-permute-start(f32[512,512]{1,0:T(8,128)} %add.985), channel_id=1, source_target_pairs={{0,1},{1,2},{2,3},{3,4},{4,5},{5,6},{6,7},{7,8},{8,9},{9,10},{10,1... | collective-permute-start | bytes 3145736 | tf_op jit(solution)/shard_map/while/body/eval_jaxpr/ppermute | solution.py:15
  1036.7 11.7 collective-permute-start.2
  1081.0 13.4 collective-permute-start.3
  1103.0 27.4 %collective-permute-start.6 = (f32[512,512]{1,0:T(8,128)}, f32[512,512]{1,0:T(8,128)}, u32[]{:S(2)}, u32[]{:S(2)}) collective-permute-start(f32[512,512]{1,0:T(8,128)} %add.989), channel_id=1, source_target_pairs={{0,1},{1,2},{2,3},{3,4},{4,5},{5,6},{6,7},{7,8},{8,9},{9,10},{10,1... | collective-permute-start | bytes 3145736 | tf_op jit(solution)/shard_map/while/body/eval_jaxpr/ppermute | solution.py:15
  1132.8 20.5 %collective-permute-start.7 = (f32[512,512]{1,0:T(8,128)}, f32[512,512]{1,0:T(8,128)}, u32[]{:S(2)}, u32[]{:S(2)}) collective-permute-start(f32[512,512]{1,0:T(8,128)} %add.993), channel_id=1, source_target_pairs={{0,1},{1,2},{2,3},{3,4},{4,5},{5,6},{6,7},{7,8},{8,9},{9,10},{10,1... | collective-permute-start | bytes 3145736 | tf_op jit(solution)/shard_map/while/body/eval_jaxpr/ppermute | solution.py:15
  1155.9 20.7 %collective-permute-start = (bf16[512,512]{1,0:T(8,128)(2,1)S(1)}, bf16[512,512]{1,0:T(8,128)(2,1)S(1)}, u32[]{:S(2)}, u32[]{:S(2)}) collective-permute-start(bf16[512,512]{1,0:T(8,128)(2,1)S(1)} %get-tuple-element.623), channel_id=1, source_target_pairs={{0,1},{1,2},{2,3},{3,4},{4,5},{5,6},{6,7},{7,8},{8,9},{9,10},{10,1... | collective-permute-start | bytes 1572872 | tf_op jit(solution)/shard_map/while/body/eval_jaxpr/ppermute | solution.py:15
  1158.2 112.1 %collective-permute-start.4 = (f32[512,512]{1,0:T(8,128)}, f32[512,512]{1,0:T(8,128)}, u32[]{:S(2)}, u32[]{:S(2)}) collective-permute-start(f32[512,512]{1,0:T(8,128)} %broadcast_select_fusion.2), channel_id=1, source_target_pairs={{0,1},{1,2},{2,3},{3,4},{4,5},{5,6},{6,7},{7,8},{8,9},{9,10},{10,1... | collective-permute-start | bytes 3145736 | tf_op jit(solution)/shard_map/while/body/eval_jaxpr/ppermute | solution.py:15
  1222.4 11.7 collective-permute-start.1
  1272.8 71.8 %collective-permute-start.5 = (f32[512,512]{1,0:T(8,128)}, f32[512,512]{1,0:T(8,128)}, u32[]{:S(2)}, u32[]{:S(2)}) collective-permute-start(f32[512,512]{1,0:T(8,128)} %add.985), channel_id=1, source_target_pairs={{0,1},{1,2},{2,3},{3,4},{4,5},{5,6},{6,7},{7,8},{8,9},{9,10},{10,1... | collective-permute-start | bytes 3145736 | tf_op jit(solution)/shard_map/while/body/eval_jaxpr/ppermute | solution.py:15
  1272.8 22.7 %collective-permute-start.2 = (bf16[512,512]{1,0:T(8,128)(2,1)S(1)}, bf16[512,512]{1,0:T(8,128)(2,1)S(1)}, u32[]{:S(2)}, u32[]{:S(2)}) collective-permute-start(bf16[512,512]{1,0:T(8,128)(2,1)S(1)} %collective-permute-done.1), channel_id=1, source_target_pairs={{0,1},{1,2},{2,3},{3,4},{4,5},{5,6},{6,7},{7,8},{8,9},{9,10},{10,1... | collective-permute-start | bytes 1572872 | tf_op jit(solution)/shard_map/while/body/eval_jaxpr/ppermute | solution.py:15
  1328.2 11.3 collective-permute-start.3
  1347.6 24.3 %collective-permute-start.6 = (f32[512,512]{1,0:T(8,128)}, f32[512,512]{1,0:T(8,128)}, u32[]{:S(2)}, u32[]{:S(2)}) collective-permute-start(f32[512,512]{1,0:T(8,128)} %add.989), channel_id=1, source_target_pairs={{0,1},{1,2},{2,3},{3,4},{4,5},{5,6},{6,7},{7,8},{8,9},{9,10},{10,1... | collective-permute-start | bytes 3145736 | tf_op jit(solution)/shard_map/while/body/eval_jaxpr/ppermute | solution.py:15
  1374.4 18.0 %collective-permute-start.7 = (f32[512,512]{1,0:T(8,128)}, f32[512,512]{1,0:T(8,128)}, u32[]{:S(2)}, u32[]{:S(2)}) collective-permute-start(f32[512,512]{1,0:T(8,128)} %add.993), channel_id=1, source_target_pairs={{0,1},{1,2},{2,3},{3,4},{4,5},{5,6},{6,7},{7,8},{8,9},{9,10},{10,1... | collective-permute-start | bytes 3145736 | tf_op jit(solution)/shard_map/while/body/eval_jaxpr/ppermute | solution.py:15
  1398.1 41.8 %collective-permute-start.23 = (f32[512,512]{1,0:T(8,128)}, f32[512,512]{1,0:T(8,128)}, u32[]{:S(2)}, u32[]{:S(2)}) collective-permute-start(f32[512,512]{1,0:T(8,128)} %get-tuple-element.357), channel_id=1, source_target_pairs={{0,8},{1,9},{2,10},{3,11},{4,12},{5,13},{6,14},{7,15},{8,0},{9,1},... | collective-permute-start | bytes 3145736 | tf_op jit(solution)/shard_map/ppermute | solution.py:15
  (73 other events, 1225.8 us)
